TPU v7x, 512 devices: a whole 4x4x16 slice. The times are simulated.
512 devices in a mesh: dp: 8 (over x, core), expert: 64 (over y, z).
Axes of the slice: x: 4, y: 4, z: 16, core: 2. Of those that a mesh axis runs over, the one named last changes fastest.
Arguments:
- tokens: bfloat16 [8192, 2048], P('expert', 'dp'), may hold values from -6 to 6
- cotangent: bfloat16 [8192, 2048], P('expert', 'dp'), may hold values from -6 to 6
- routes: int32 [8192, 8], P('expert'), may hold values from 0 to 63, as said below
- mix_weights: float32 [8192, 8], P('expert'), may hold values from 0.05 to 0.5
- w_gate: bfloat16 [64, 2048, 384], P('expert', 'dp'), may hold values from -0.125 to 0.125
- w_up: bfloat16 [64, 2048, 384], P('expert', 'dp'), may hold values from -0.125 to 0.125
- w_down: bfloat16 [64, 384, 2048], P('expert', None, 'dp'), may hold values from -0.3125 to 0.3125
Outputs:
- mixed: bfloat16 [8192, 2048], P('expert', 'dp')
- token_grad: bfloat16 [8192, 2048], P('expert', 'dp')
- gate_grad: float32 [64, 2048, 384], P('expert', 'dp')
- up_grad: float32 [64, 2048, 384], P('expert', 'dp')
- down_grad: float32 [64, 384, 2048], P('expert', None, 'dp')
Inputs may be any that keep to these rules, and one draw needn't show every extreme that they name: `routes`: each row names 8 different experts. In each aligned block of 128 rows at most 32 rows name the same expert, and some block reaches that. In all, at most 1792 rows name one expert, and some expert is named by exactly that many.
All inputs are finite; a program needn't handle non-finite values.
Results may differ from a plain program's by a relative error of at most 0.023.
Values may be sent and summed in bfloat16 or wider, within the bound.
A program may use at most 64 MiB of HBM per device.

v0:
```python
import jax
import jax.numpy as jnp
from jax import lax
from jax.sharding import PartitionSpec as P


def contract(left_side, right_side, left_dim, right_dim):
    return lax.dot_general(
        left_side,
        right_side,
        (((left_dim,), (right_dim,)), ((), ())),
        preferred_element_type=jnp.float32,
    )


def silu_parts(gate_in):
    logistic = jax.nn.sigmoid(gate_in)
    return (gate_in * logistic, logistic * (1.0 + gate_in * (1.0 - logistic)))


def split_three(values):
    high = values.astype(jnp.bfloat16)
    rest = values - high.astype(jnp.float32)
    middle = rest.astype(jnp.bfloat16)
    low = (rest - middle.astype(jnp.float32)).astype(jnp.bfloat16)
    return (high, middle, low)


def shards(tokens, cotangent, routes, mix_weights, w_gate, w_up, w_down):
    tok_rows, width_dev = tokens.shape
    picks_per = routes.shape[1]
    dp_count = lax.axis_size("dp")
    owner_count = lax.axis_size("expert")
    hidden = w_gate.shape[2]
    sub_rows = tok_rows // dp_count
    width = width_dev * dp_count
    me_dp = lax.axis_index("dp")
    me_expert = lax.axis_index("expert")
    weights_dev = jnp.concatenate([w_gate[0], w_up[0], w_down[0].T], axis=1)
    weights = lax.all_gather(weights_dev, "dp", axis=0, tiled=True)
    both = jnp.stack([tokens, cotangent]).reshape(2, dp_count, sub_rows, width_dev)
    both = lax.all_to_all(both, "dp", split_axis=1, concat_axis=1, tiled=True)
    both = both.transpose(2, 0, 1, 3).reshape(sub_rows, 2 * width)
    my_routes = lax.dynamic_slice_in_dim(routes, me_dp * sub_rows, sub_rows, 0)
    my_mix = lax.dynamic_slice_in_dim(mix_weights, me_dp * sub_rows, sub_rows, 0)
    extra = jnp.concatenate([my_routes.astype(jnp.bfloat16), *split_three(my_mix)], axis=1)
    extra = jnp.pad(extra, ((0, 0), (0, 128 - extra.shape[1])))
    rows = lax.all_gather(jnp.concatenate([both, extra], axis=1), "expert", axis=0, tiled=True)
    x_rows = rows[:, :width]
    c_rows = rows[:, width : 2 * width]
    tail = rows[:, 2 * width : 2 * width + 4 * picks_per].astype(jnp.float32)
    tail = tail.reshape(-1, 4, picks_per)
    mix_all = tail[:, 1] + tail[:, 2] + tail[:, 3]
    named = tail[:, 0] == me_expert.astype(jnp.float32)
    weight_row = jnp.sum(jnp.where(named, mix_all, 0.0), axis=1, keepdims=True)
    w_in = weights[:, : 2 * hidden]
    w_out = weights[:, 2 * hidden :]
    pre = contract(x_rows, w_in, 1, 0)
    back_hidden = contract(c_rows, w_out, 1, 0) * weight_row
    gate_in, up_in = (pre[:, :hidden], pre[:, hidden:])
    activated, slope_silu = silu_parts(gate_in)
    hidden_mix = (activated * up_in * weight_row).astype(jnp.bfloat16)
    gate_back = (back_hidden * up_in * slope_silu).astype(jnp.bfloat16)
    up_back = (back_hidden * activated).astype(jnp.bfloat16)
    in_back = jnp.concatenate([gate_back, up_back], axis=1)
    mixed_part = contract(hidden_mix, w_out, 1, 1).astype(jnp.bfloat16)
    grad_part = contract(in_back, w_in, 1, 1).astype(jnp.bfloat16)
    sums = lax.psum_scatter(
        jnp.concatenate([mixed_part, grad_part], axis=1), "expert", scatter_dimension=0, tiled=True
    )
    in_grad = contract(x_rows, in_back, 0, 0).astype(jnp.bfloat16)
    out_grad = contract(c_rows, hidden_mix, 0, 0).astype(jnp.bfloat16)
    weight_grads = lax.psum_scatter(
        jnp.concatenate([in_grad, out_grad], axis=1), "dp", scatter_dimension=0, tiled=True
    ).astype(jnp.float32)
    sums = sums.reshape(sub_rows, 2, dp_count, width_dev).transpose(1, 2, 0, 3)
    sums = lax.all_to_all(sums, "dp", split_axis=1, concat_axis=1, tiled=True)
    sums = sums.reshape(2, tok_rows, width_dev)
    return (
        sums[0],
        sums[1],
        weight_grads[None, :, :hidden],
        weight_grads[None, :, hidden : 2 * hidden],
        weight_grads[:, 2 * hidden :].T[None],
    )


def solution(mesh):
    placed = (
        P("expert", "dp"),
        P("expert", "dp"),
        P("expert", None),
        P("expert", None),
        P("expert", "dp", None),
        P("expert", "dp", None),
        P("expert", None, "dp"),
    )
    return jax.shard_map(
        shards,
        mesh=mesh,
        in_specs=placed,
        out_specs=(
            P("expert", "dp"),
            P("expert", "dp"),
            P("expert", "dp", None),
            P("expert", "dp", None),
            P("expert", None, "dp"),
        ),
        check_vma=False,
    )
```

profile of v0, /device:TPU:1, one launch (start us, length us, event | category | flops | bytes accessed | tf_op | source)
XLA Modules:
  0.0 1037.5 jit_solution(6336059974394394952)
XLA Ops:
  7.2 0.9 pad_maximum_fusion.6
  8.1 0.8 copy.61
  8.8 10.1 all-to-all-start
  19.0 0.0 all-gather.3.cloned.1.call-start
  19.0 0.8 subtract_convert_fusion
  19.8 0.8 dynamic-slice_convert_fusion
  20.6 0.1 copy.75
  20.7 3.6 all-to-all-done
  24.2 0.1 copy.62
  24.4 0.7 fusion.23
  25.0 0.0 all-gather.3.cloned.1.call-update
  25.0 0.0 all-gather.5.cloned.1.call-start
  25.1 1.1 copy.64
  26.2 1.1 copy.65
  27.2 1.8 pad_maximum_fusion.5
  29.0 0.0 all-gather.5.cloned.1.call-update
  29.1 0.0 reduce-scatter.5.cloned.1.call-start
  29.1 143.9 %all-gather.3.cloned.1.call-done = bf16[1024,4224]{1,0:T(8,128)(2,1)} async-done(((bf16[16,4224]{1,0:T(8,128)(2,1)}), bf16[1024,4224]{1,0:T(8,128)(2,1)}) %all-gather.3.cloned.1.call-update) | async-done | bytes 8650768 | tf_op jit(solution)/shard_map/all_gather | solution.py:48
  173.1 1.0 slice.70
  174.0 0.1 copy.72
  174.2 49.0 %all-gather.5.cloned.1.call-done = bf16[2048,1152]{0,1:T(8,128)(2,1)} async-done(((bf16[256,1152]{0,1:T(8,128)(2,1)}), bf16[2048,1152]{0,1:T(8,128)(2,1)}) %all-gather.5.cloned.1.call-update) | async-done | bytes 4718608 | tf_op jit(solution)/shard_map/all_gather | solution.py:40
  223.2 6.3 fusion.6
  229.5 0.0 slice-start.2
  229.5 5.2 multiply_convert_fusion.1
  234.7 0.0 slice-done
  234.7 0.0 slice-done.1
  234.7 1.8 fusion.11
  236.5 3.6 fusion.8
  240.2 2.5 pad_maximum_fusion.1
  242.7 0.0 reduce-scatter.5.cloned.1.call-update
  242.7 0.2 reduce-scatter.3.cloned.1.call-start
  242.9 5.8 convolution_convert_fusion
  248.7 6.9 convolution_convert_fusion.1
  255.7 7.9 pad_maximum_fusion
  263.6 0.0 reduce-scatter.3.cloned.1.call-update
  263.6 24.4 %reduce-scatter.5.cloned.1.call-done = bf16[256,1152]{0,1:T(8,128)(2,1)} async-done(((bf16[2048,1152]{0,1:T(8,128)(2,1)}), bf16[256,1152]{0,1:T(8,128)(2,1)}) %reduce-scatter.5.cloned.1.call-update) | async-done | bytes 589840 | tf_op jit(solution)/shard_map/reduce_scatter | solution.py:73
  288.1 1.1 convert_element_type.62
  289.2 718.3 %reduce-scatter.3.cloned.1.call-done = bf16[16,4096]{1,0:T(8,128)(2,1)} async-done(((bf16[1024,4096]{1,0:T(8,128)(2,1)}), bf16[16,4096]{1,0:T(8,128)(2,1)}) %reduce-scatter.3.cloned.1.call-update) | async-done | bytes 131088 | tf_op jit(solution)/shard_map/reduce_scatter | solution.py:68
  1007.5 0.9 copy.77
  1008.5 0.8 copy.79
  1009.2 15.0 %all-to-all-start.1 = ((bf16[2,8,16,256]{3,0,2,1:T(2,128)(2,1)}), bf16[2,8,16,256]{3,0,2,1:T(2,128)(2,1)S(1)}, u32[]{:S(2)}, u32[]{:S(2)}) async-start(bf16[2,8,16,256]{3,0,2,1:T(2,128)(2,1)} %bitcast.31), calls=%async_computation.2 | async-start | bytes 262144 | tf_op jit(solution)/shard_map/all_to_all | solution.py:77
  1024.2 0.8 slice_bitcast_fusion
  1025.1 0.9 copy.71
  1026.0 0.9 copy.70
  1026.9 2.6 all-to-all-done.1
  1029.5 0.2 fusion.30
  1029.7 0.6 copy.74
  1030.4 0.6 copy.73
  (8 shorter events, 0.1 us)
Async XLA Ops:
  8.8 15.4 %all-to-all-start = ((bf16[2,8,16,256]{3,0,2,1:T(2,128)(2,1)}), bf16[2,8,16,256]{3,0,2,1:T(2,128)(2,1)S(1)}, u32[]{:S(2)}, u32[]{:S(2)}) async-start(bf16[2,8,16,256]{3,0,2,1:T(2,128)(2,1)} %copy.61), calls=%async_computation | async-start | bytes 262144 | tf_op jit(solution)/shard_map/all_to_all | solution.py:42
  19.0 154.1 %all-gather.3.cloned.1.call-start = ((), (), s32[]{:S(2)}) async-start(), calls=%async_computation.4 | async-start | bytes 8785920 | tf_op jit(solution)/shard_map/all_gather | solution.py:48
  25.0 198.1 %all-gather.5.cloned.1.call-start = ((), (), s32[]{:S(2)}) async-start(), calls=%async_computation.5 | async-start | bytes 5308416 | tf_op jit(solution)/shard_map/all_gather | solution.py:40
  29.1 259.0 %reduce-scatter.5.cloned.1.call-start = ((), (), s32[]{:S(2)}) async-start(), calls=%async_computation.7 | async-start | bytes 5308416 | tf_op jit(solution)/shard_map/reduce_scatter | solution.py:73
  223.2 11.5 %slice-start = ((s8[8650752]{0:T(1024)(128)(4,1)}), s8[4194304]{0:T(1024)(128)(4,1)S(1)}, s32[]{:S(2)}) async-start(s8[8650752]{0:T(1024)(128)(4,1)} %bitcast.44), calls=%async_computation.8 | async-start | bytes 8388608
  223.2 11.5 %slice-start.1 = ((s8[8650752]{0:T(1024)(128)(4,1)}), s8[4194304]{0:T(1024)(128)(4,1)S(1)}, s32[]{:S(2)}) async-start(s8[8650752]{0:T(1024)(128)(4,1)} %bitcast.44), calls=%async_computation.9 | async-start | bytes 8388608
  229.5 5.2 slice-start.2
  242.7 764.8 %reduce-scatter.3.cloned.1.call-start = ((), (), s32[]{:S(2)}) async-start(), calls=%async_computation.6 | async-start | bytes 8519680 | tf_op jit(solution)/shard_map/reduce_scatter | solution.py:68
  1009.2 20.3 %all-to-all-start.1 = ((bf16[2,8,16,256]{3,0,2,1:T(2,128)(2,1)}), bf16[2,8,16,256]{3,0,2,1:T(2,128)(2,1)S(1)}, u32[]{:S(2)}, u32[]{:S(2)}) async-start(bf16[2,8,16,256]{3,0,2,1:T(2,128)(2,1)} %bitcast.31), calls=%async_computation.2 | async-start | bytes 262144 | tf_op jit(solution)/shard_map/all_to_all | solution.py:77
Sparse Core Ops, SparseCore 0:
  25.2 147.8 all-gather.2
  175.2 47.9 all-gather.4
  242.8 45.1 reduce-scatter.4
  292.4 715.1 reduce-scatter.2
where the time goes:
time: 1040 us
  waiting for transfers between devices  942 us (91%)
  matrix products  29.7 us (3%)
  starting transfers between devices  25.4 us (2%)
  other arithmetic  16.6 us (2%)
  between operations  13.9 us (1%)
    reduce_scatter x1, waiting for transfers between devices, shards(): lax.psum_scatter(jnp.concatenate([mixed_part, grad_part], axis=1), 'exper...  718 us
    all_gather x1, waiting for transfers between devices, shards(): lax.all_gather(jnp.concatenate([both, extra], axis=1), 'expert', axis=0,...  144 us
    all_gather x1, waiting for transfers between devices, shards(): weights = lax.all_gather(weights_dev, 'dp', axis=0, tiled=True)  49 us
    dot_general x6, matrix products, contract(): lax.dot_general(left_side, right_side, (((left_dim,), (right_dim,)), ((),...  29.7 us
    reduce_scatter x1, waiting for transfers between devices, shards(): lax.psum_scatter(jnp.concatenate([in_grad, out_grad], axis=1), 'dp', scat...  24.4 us
  transfers between devices with their start and end apart: 6, of which 6 were waited for; matrix products, arithmetic and copies ran while one was open for 3% of the time, Pallas kernels for 0%

commit v1 on v0

--- a/solution.py
+++ b/solution.py
@@ -45,7 +45,15 @@
     my_mix = lax.dynamic_slice_in_dim(mix_weights, me_dp * sub_rows, sub_rows, 0)
     extra = jnp.concatenate([my_routes.astype(jnp.bfloat16), *split_three(my_mix)], axis=1)
     extra = jnp.pad(extra, ((0, 0), (0, 128 - extra.shape[1])))
-    rows = lax.all_gather(jnp.concatenate([both, extra], axis=1), "expert", axis=0, tiled=True)
+    rows = jnp.concatenate(
+        lax.all_to_all(
+            jnp.stack([jnp.concatenate([both, extra], axis=1)] * lax.axis_size("expert")),
+            "expert",
+            0,
+            0,
+        ),
+        axis=0,
+    )
     x_rows = rows[:, :width]
     c_rows = rows[:, width : 2 * width]
     tail = rows[:, 2 * width : 2 * width + 4 * picks_per].astype(jnp.float32)

time: 1040 us -> 1230 us (1.18)
  waiting for transfers between devices: 942 us -> 1120 us
  starting transfers between devices: 25.4 us -> 39.9 us
    all_to_all x0 -> x1, waiting for transfers between devices: none -> 376 us  [shards(): lax.all_to_all(jnp.stack([jnp.concatenate([both, extra], axis=1)] * lax.a...]
    all_gather x1 -> x0, waiting for transfers between devices: 144 us -> none  [shards(): lax.all_gather(jnp.concatenate([both, extra], axis=1), 'expert', axis=0,...]
    all_gather x1, waiting for transfers between devices: 49 us -> 0.02 us  [shards(): weights = lax.all_gather(weights_dev, 'dp', axis=0, tiled=True)]
    all_to_all x0 -> x1, starting transfers between devices: none -> 14.5 us  [shards(): lax.all_to_all(jnp.stack([jnp.concatenate([both, extra], axis=1)] * lax.a...]
  transfers between devices with their start and end apart: 6 -> 6, of which waited for: 6 -> 5; matrix products, arithmetic and copies ran while one was open for 3% -> 2% of each run, Pallas kernels for 0% -> 0%
where the time goes in v1:
time: 1230 us
  waiting for transfers between devices  1120 us (91%)
  starting transfers between devices  39.9 us (3%)
  matrix products  34.6 us (3%)
  other arithmetic  15.1 us (1%)
  between operations  13.9 us (1%)
    reduce_scatter x1, waiting for transfers between devices, shards(): lax.psum_scatter(jnp.concatenate([mixed_part, grad_part], axis=1), 'exper...  719 us
    all_to_all x1, waiting for transfers between devices, shards(): lax.all_to_all(jnp.stack([jnp.concatenate([both, extra], axis=1)] * lax.a...  376 us
    dot_general x6, matrix products, contract(): lax.dot_general(left_side, right_side, (((left_dim,), (right_dim,)), ((),...  34.6 us
  transfers between devices with their start and end apart: 6, of which 5 were waited for; matrix products, arithmetic and copies ran while one was open for 2% of the time, Pallas kernels for 0%

profile of v1, /device:TPU:1, one launch (start us, length us, event | category | flops | bytes accessed | tf_op | source)
XLA Modules:
  0.0 1233.6 jit_solution(4600604086334493116)
XLA Ops:
  7.2 0.9 pad_maximum_fusion.6
  8.1 0.8 copy.62
  8.8 10.1 all-to-all-start
  19.0 0.8 subtract_convert_fusion
  19.8 0.8 dynamic-slice_convert_fusion
  20.6 0.1 copy.76
  20.6 3.6 all-to-all-done
  24.2 0.1 copy.63
  24.4 3.9 stack.11
  28.3 0.0 copy-start.1
  28.3 14.5 %all-to-all-start.1 = ((bf16[64,16,4224]{2,1,0:T(8,128)(2,1)}), bf16[64,16,4224]{2,1,0:T(8,128)(2,1)}, u32[]{:S(2)}, u32[]{:S(2)}) async-start(bf16[64,16,4224]{2,1,0:T(8,128)(2,1)} %stack.11), calls=%async_computation.1 | async-start | bytes 17301504 | tf_op jit(solution)/shard_map/all_to_all | solution.py:49
  42.8 0.0 all-gather.2.cloned.1.call-start
  42.8 0.0 copy-done.1
  42.8 0.1 copy.65
  43.0 0.0 copy-done.2
  43.0 0.1 copy.66
  43.1 0.0 copy-done
  43.1 0.9 pad_maximum_fusion.5
  44.0 0.0 all-gather.2.cloned.1.call-update
  44.1 0.0 reduce-scatter.5.cloned.1.call-start
  44.1 375.9 %all-to-all-done.1 = bf16[64,16,4224]{2,1,0:T(8,128)(2,1)} async-done(((bf16[64,16,4224]{2,1,0:T(8,128)(2,1)}), bf16[64,16,4224]{2,1,0:T(8,128)(2,1)}, u32[]{:S(2)}, u32[]{:S(2)}) %all-to-all-start.1) | async-done | bytes 8650784 | tf_op jit(solution)/shard_map/all_to_all | solution.py:49
  420.0 1.0 slice.70
  421.0 0.1 copy.73
  421.2 0.0 all-gather.2.cloned.1.call-done
  421.2 6.2 fusion.6
  427.4 5.1 multiply_convert_fusion.1
  432.5 4.0 fusion.11
  436.5 6.5 fusion.8
  443.0 2.6 pad_maximum_fusion.1
  445.6 0.0 reduce-scatter.5.cloned.1.call-update
  445.6 0.2 reduce-scatter.3.cloned.1.call-start
  445.8 5.9 convolution_convert_fusion
  451.7 6.9 convolution_convert_fusion.1
  458.6 7.9 pad_maximum_fusion
  466.5 0.0 reduce-scatter.3.cloned.1.call-update
  466.6 17.1 %reduce-scatter.5.cloned.1.call-done = bf16[256,1152]{0,1:T(8,128)(2,1)} async-done(((bf16[2048,1152]{0,1:T(8,128)(2,1)}), bf16[256,1152]{0,1:T(8,128)(2,1)}) %reduce-scatter.5.cloned.1.call-update) | async-done | bytes 589840 | tf_op jit(solution)/shard_map/reduce_scatter | solution.py:81
  483.7 1.1 convert_element_type.62
  484.8 718.7 %reduce-scatter.3.cloned.1.call-done = bf16[16,4096]{1,0:T(8,128)(2,1)} async-done(((bf16[1024,4096]{1,0:T(8,128)(2,1)}), bf16[16,4096]{1,0:T(8,128)(2,1)}) %reduce-scatter.3.cloned.1.call-update) | async-done | bytes 131088 | tf_op jit(solution)/shard_map/reduce_scatter | solution.py:76
  1203.6 0.9 copy.78
  1204.5 0.8 copy.80
  1205.3 15.0 %all-to-all-start.2 = ((bf16[2,8,16,256]{3,0,2,1:T(2,128)(2,1)}), bf16[2,8,16,256]{3,0,2,1:T(2,128)(2,1)S(1)}, u32[]{:S(2)}, u32[]{:S(2)}) async-start(bf16[2,8,16,256]{3,0,2,1:T(2,128)(2,1)} %bitcast.32), calls=%async_computation.3 | async-start | bytes 262144 | tf_op jit(solution)/shard_map/all_to_all | solution.py:85
  1220.3 0.8 slice_bitcast_fusion
  1221.1 0.9 copy.71
  1222.0 0.9 copy.72
  1222.9 2.6 all-to-all-done.2
  1225.5 0.2 fusion.30
  1225.8 0.6 copy.74
  1226.4 0.6 copy.75
  (7 shorter events, 0.1 us)
Async XLA Ops:
  8.8 15.4 %all-to-all-start = ((bf16[2,8,16,256]{3,0,2,1:T(2,128)(2,1)}), bf16[2,8,16,256]{3,0,2,1:T(2,128)(2,1)S(1)}, u32[]{:S(2)}, u32[]{:S(2)}) async-start(bf16[2,8,16,256]{3,0,2,1:T(2,128)(2,1)} %copy.62), calls=%async_computation | async-start | bytes 262144 | tf_op jit(solution)/shard_map/all_to_all | solution.py:42
  28.3 14.5 %copy-start.1 = (bf16[1,256,384]{2,1,0:T(8,128)(2,1)S(1)}, bf16[1,256,384]{2,1,0:T(8,128)(2,1)}, u32[]{:S(2)}) copy-start(bf16[1,256,384]{2,1,0:T(8,128)(2,1)} %param.11) | copy-start | bytes 589828
  28.3 14.7 %copy-start.2 = (bf16[1,256,384]{2,1,0:T(8,128)(2,1)S(1)}, bf16[1,256,384]{2,1,0:T(8,128)(2,1)}, u32[]{:S(2)}) copy-start(bf16[1,256,384]{2,1,0:T(8,128)(2,1)} %param.12) | copy-start | bytes 589828
  28.3 14.8 %copy-start = (bf16[1,384,256]{2,1,0:T(8,128)(2,1)S(1)}, bf16[1,384,256]{2,1,0:T(8,128)(2,1)}, u32[]{:S(2)}) copy-start(bf16[1,384,256]{2,1,0:T(8,128)(2,1)} %param.13) | copy-start | bytes 589828
  28.3 391.7 %all-to-all-start.1 = ((bf16[64,16,4224]{2,1,0:T(8,128)(2,1)}), bf16[64,16,4224]{2,1,0:T(8,128)(2,1)}, u32[]{:S(2)}, u32[]{:S(2)}) async-start(bf16[64,16,4224]{2,1,0:T(8,128)(2,1)} %stack.11), calls=%async_computation.1 | async-start | bytes 17301504 | tf_op jit(solution)/shard_map/all_to_all | solution.py:49
  42.8 378.4 %all-gather.2.cloned.1.call-start = ((), (), s32[]{:S(2)}) async-start(), calls=%async_computation.5 | async-start | bytes 5308416 | tf_op jit(solution)/shard_map/all_gather | solution.py:40
  44.1 439.6 %reduce-scatter.5.cloned.1.call-start = ((), (), s32[]{:S(2)}) async-start(), calls=%async_computation.7 | async-start | bytes 5308416 | tf_op jit(solution)/shard_map/reduce_scatter | solution.py:81
  445.6 758.0 %reduce-scatter.3.cloned.1.call-start = ((), (), s32[]{:S(2)}) async-start(), calls=%async_computation.6 | async-start | bytes 8519680 | tf_op jit(solution)/shard_map/reduce_scatter | solution.py:76
  1205.3 20.2 %all-to-all-start.2 = ((bf16[2,8,16,256]{3,0,2,1:T(2,128)(2,1)}), bf16[2,8,16,256]{3,0,2,1:T(2,128)(2,1)S(1)}, u32[]{:S(2)}, u32[]{:S(2)}) async-start(bf16[2,8,16,256]{3,0,2,1:T(2,128)(2,1)} %bitcast.32), calls=%async_computation.3 | async-start | bytes 262144 | tf_op jit(solution)/shard_map/all_to_all | solution.py:85
Sparse Core Ops, SparseCore 0:
  45.7 45.2 all-gather.1
  445.7 37.9 reduce-scatter.4
  488.2 715.3 reduce-scatter.2
